TPU v7x, 32 devices: a whole 2x2x4 slice. The times are simulated.
32 devices in a mesh: fsdp: 4 (over y, x), ctx: 4 (over z), tp: 2 (over core).
Axes of the slice: x: 2, y: 2, z: 4, core: 2. Of those that a mesh axis runs over, the one named last changes fastest.
Arguments:
- inputs: bfloat16 [4, 1024, 2048], P('fsdp', 'ctx'), may hold values from -6 to 6
- positions: int32 [4, 1024], P('fsdp', 'ctx'), may hold values from 0 to 1535, as said below
- blocks: int32 [4, 1024], P('fsdp', 'ctx'), may hold values from 0 to 7, never falling along the last dimension, each value on 1 to 256 neighbouring positions
- cotangent: bfloat16 [4, 1024, 2048], P('fsdp', 'ctx'), may hold values from -6 to 6
- attn_gain: bfloat16 [2048], P('fsdp'), may hold values from 0.099609375 to 1.8984375
- w_query: bfloat16 [2048, 2048], P('fsdp', 'tp'), may hold values from -0.125 to 0.125
- w_key: bfloat16 [2048, 256], P('fsdp', 'tp'), may hold values from -0.125 to 0.125
- w_value: bfloat16 [2048, 256], P('fsdp', 'tp'), may hold values from -0.125 to 0.125
- w_out: bfloat16 [2048, 2048], P('tp', 'fsdp'), may hold values from -1 to 1
- mlp_gain: bfloat16 [2048], P('fsdp'), may hold values from 0.099609375 to 1.8984375
- w_gate: bfloat16 [2048, 5632], P('fsdp', 'tp'), may hold values from -0.125 to 0.125
- w_up: bfloat16 [2048, 5632], P('fsdp', 'tp'), may hold values from -0.125 to 0.125
- w_down: bfloat16 [5632, 2048], P('tp', 'fsdp'), may hold values from -0.078125 to 0.078125
Outputs:
- output: bfloat16 [4, 1024, 2048], P('fsdp', 'ctx')
- input_grad: float32 [4, 1024, 2048], P('fsdp', 'ctx')
- attn_gain_grad: float32 [2048], P('fsdp')
- query_grad: float32 [2048, 2048], P('fsdp', 'tp')
- key_grad: float32 [2048, 256], P('fsdp', 'tp')
- value_grad: float32 [2048, 256], P('fsdp', 'tp')
- out_grad: float32 [2048, 2048], P('tp', 'fsdp')
- mlp_gain_grad: float32 [2048], P('fsdp')
- gate_grad: float32 [2048, 5632], P('fsdp', 'tp')
- up_grad: float32 [2048, 5632], P('fsdp', 'tp')
- down_grad: float32 [5632, 2048], P('tp', 'fsdp')
Inputs may be any that keep to these rules, and one draw needn't show every extreme that they name: `positions`: positions start at 0 and rise by 1 or 2 from each token to the next along a sequence; in every sequence exactly 512 of these steps are 2. `blocks`: block ids never fall along a sequence; every block holds 1 to 256 tokens.
All inputs are finite; a program needn't handle non-finite values.
Results may differ from a plain program's by a relative error of at most 0.023.
Values may be sent and summed in bfloat16 or wider, within the bound.
A program may use at most 320 MiB of HBM per device.

v0:
```python
import math
import jax
import jax.numpy as jnp
from jax import lax
from jax.sharding import PartitionSpec as P

HD = 64
EPSILON = 1e-05
NEGATIVE = -1e30


def angles(positions, head_size):
    half_size = head_size // 2
    frequency = jnp.exp(
        jnp.arange(half_size, dtype=jnp.float32) * (-2.0 * math.log(10000.0) / head_size)
    )
    turned = positions.astype(jnp.float32)[:, None] * frequency[None, :]
    return (jnp.cos(turned)[:, None, :], jnp.sin(turned)[:, None, :])


def rotate(values, cosine, sine_turn):
    half_size = values.shape[-1] // 2
    first_half = values[..., :half_size]
    second_half = values[..., half_size:]
    return jnp.concatenate(
        [
            first_half * cosine - second_half * sine_turn,
            second_half * cosine + first_half * sine_turn,
        ],
        axis=-1,
    )


def masked_scores(query_four, key_block, key_ids, query_ids, factor):
    scores = (
        jnp.einsum("tkgd,skd->kgts", query_four, key_block, preferred_element_type=jnp.float32)
        * factor
    )
    allowed = key_ids[None, :] <= query_ids[:, None]
    return (jnp.where(allowed, scores, NEGATIVE), allowed)


def norm_back(upstream, normed, scale, gain):
    weighted = upstream * gain
    return scale * (weighted - normed * jnp.mean(weighted * normed, axis=-1, keepdims=True))


def local(
    inputs,
    positions,
    blocks,
    cotangent,
    attn_gain,
    w_query,
    w_key,
    w_value,
    w_out,
    mlp_gain,
    w_gate,
    w_up,
    w_down,
):
    token_rows = inputs[0].astype(jnp.float32)
    place_row = positions[0]
    own_ids = blocks[0]
    back_low = cotangent[0]
    back_full = back_low.astype(jnp.float32)
    tokens = token_rows.shape[0]
    gain_one, query_w, key_w, value_w, gain_two, gate_w, up_w = (
        lax.all_gather(attn_gain, "fsdp", axis=0, tiled=True),
        lax.all_gather(w_query, "fsdp", axis=0, tiled=True),
        lax.all_gather(w_key, "fsdp", axis=0, tiled=True),
        lax.all_gather(w_value, "fsdp", axis=0, tiled=True),
        lax.all_gather(mlp_gain, "fsdp", axis=0, tiled=True),
        lax.all_gather(w_gate, "fsdp", axis=0, tiled=True),
        lax.all_gather(w_up, "fsdp", axis=0, tiled=True),
    )
    out_w, down_w = (
        lax.all_gather(w_out, "fsdp", axis=1, tiled=True),
        lax.all_gather(w_down, "fsdp", axis=1, tiled=True),
    )
    gain_one = gain_one.astype(jnp.float32)
    gain_two = gain_two.astype(jnp.float32)
    scale_one = lax.rsqrt(jnp.mean(token_rows * token_rows, axis=-1, keepdims=True) + EPSILON)
    normed_one = token_rows * scale_one
    input_one = (normed_one * gain_one).astype(jnp.bfloat16)
    query_pre = jnp.dot(input_one, query_w, preferred_element_type=jnp.float32)
    key_pre = jnp.dot(input_one, key_w, preferred_element_type=jnp.float32)
    value_low = jnp.dot(input_one, value_w, preferred_element_type=jnp.float32).astype(jnp.bfloat16)
    cosine, sine_turn = angles(place_row, HD)
    query_rot = rotate(query_pre.reshape(tokens, -1, HD), cosine, sine_turn).astype(jnp.bfloat16)
    key_rot = rotate(key_pre.reshape(tokens, -1, HD), cosine, sine_turn).astype(jnp.bfloat16)
    kv_heads = key_rot.shape[1]
    grouping = query_rot.shape[1] // kv_heads
    query_four = query_rot.reshape(tokens, kv_heads, grouping, HD)
    all_keys, all_values, all_ids = (
        lax.all_gather(key_rot.reshape(tokens, kv_heads * HD), "ctx", axis=0, tiled=True),
        lax.all_gather(value_low, "ctx", axis=0, tiled=True),
        lax.all_gather(own_ids, "ctx", axis=0, tiled=True),
    )
    length = all_keys.shape[0]
    block_rows = math.gcd(length, 512)
    block_total = length // block_rows
    key_blocks = all_keys.reshape(block_total, block_rows, kv_heads, HD)
    value_blocks = all_values.reshape(block_total, block_rows, kv_heads, HD)
    id_blocks = all_ids.reshape(block_total, block_rows)
    factor = 1.0 / math.sqrt(HD)

    def stats_step(carry_pair, block_item):
        running_top, running_sum = carry_pair
        key_block, key_ids = block_item
        scores, allowed = masked_scores(query_four, key_block, key_ids, own_ids, factor)
        new_top = jnp.maximum(running_top, jnp.max(scores, axis=-1))
        fresh = jnp.where(allowed, jnp.exp(scores - new_top[..., None]), 0.0)
        new_sum = running_sum * jnp.exp(running_top - new_top) + jnp.sum(fresh, axis=-1)
        return ((new_top, new_sum), None)

    start_top = jnp.full((kv_heads, grouping, tokens), NEGATIVE, jnp.float32)
    (row_top, row_sum), _ = lax.scan(
        stats_step, (start_top, jnp.zeros_like(start_top)), (key_blocks, id_blocks)
    )

    def probabilities(key_block, key_ids):
        scores, allowed = masked_scores(query_four, key_block, key_ids, own_ids, factor)
        return jnp.where(allowed, jnp.exp(scores - row_top[..., None]) / row_sum[..., None], 0.0)

    def value_step(mixed_sum, block_item):
        key_block, value_block, key_ids = block_item
        weights_low = probabilities(key_block, key_ids).astype(jnp.bfloat16)
        return (
            mixed_sum
            + jnp.einsum(
                "kgts,skd->tkgd", weights_low, value_block, preferred_element_type=jnp.float32
            ),
            None,
        )

    attended, _ = lax.scan(
        value_step,
        jnp.zeros((tokens, kv_heads, grouping, HD), jnp.float32),
        (key_blocks, value_blocks, id_blocks),
    )
    attended_low = attended.astype(jnp.bfloat16).reshape(tokens, -1)
    hidden = token_rows + lax.psum(
        jnp.dot(attended_low, out_w, preferred_element_type=jnp.float32).astype(jnp.bfloat16), "tp"
    ).astype(jnp.float32)
    scale_two = lax.rsqrt(jnp.mean(hidden * hidden, axis=-1, keepdims=True) + EPSILON)
    normed_two = hidden * scale_two
    input_two = (normed_two * gain_two).astype(jnp.bfloat16)
    gate = jnp.dot(input_two, gate_w, preferred_element_type=jnp.float32)
    up_proj = jnp.dot(input_two, up_w, preferred_element_type=jnp.float32)
    sigmoid_gate = jax.nn.sigmoid(gate)
    silu_gate = gate * sigmoid_gate
    activation = (silu_gate * up_proj).astype(jnp.bfloat16)
    mlp_sum = lax.psum(
        jnp.dot(activation, down_w, preferred_element_type=jnp.float32).astype(jnp.bfloat16), "tp"
    ).astype(jnp.float32)
    output = (hidden + mlp_sum).astype(jnp.bfloat16)
    act_grad = jnp.einsum("td,fd->tf", back_low, down_w, preferred_element_type=jnp.float32)
    down_grad_t = jnp.einsum("td,tf->df", back_low, activation, preferred_element_type=jnp.float32)
    gate_back = (act_grad * up_proj * sigmoid_gate * (1.0 + gate * (1.0 - sigmoid_gate))).astype(
        jnp.bfloat16
    )
    up_back = (act_grad * silu_gate).astype(jnp.bfloat16)
    gate_grad = jnp.einsum("td,tf->df", input_two, gate_back, preferred_element_type=jnp.float32)
    up_grad = jnp.einsum("td,tf->df", input_two, up_back, preferred_element_type=jnp.float32)
    two_partial = jnp.einsum(
        "tf,df->td", gate_back, gate_w, preferred_element_type=jnp.float32
    ) + jnp.einsum("tf,df->td", up_back, up_w, preferred_element_type=jnp.float32)
    input_two_grad = lax.psum(two_partial.astype(jnp.bfloat16), "tp").astype(jnp.float32)
    gain_two_grad = jnp.sum(input_two_grad * normed_two, axis=0)
    hidden_grad = back_full + norm_back(input_two_grad, normed_two, scale_two, gain_two)
    hidden_low = hidden_grad.astype(jnp.bfloat16)
    out_grad_t = jnp.einsum(
        "td,tc->dc", hidden_low, attended_low, preferred_element_type=jnp.float32
    )
    attended_grad = (
        jnp.einsum("td,cd->tc", hidden_low, out_w, preferred_element_type=jnp.float32)
        .astype(jnp.bfloat16)
        .reshape(tokens, kv_heads, grouping, HD)
    )
    row_delta = jnp.einsum("tkgd,tkgd->kgt", attended_grad.astype(jnp.float32), attended)

    def back_step(query_sum, block_item):
        key_block, value_block, key_ids = block_item
        weights_full = probabilities(key_block, key_ids)
        weight_grad = jnp.einsum(
            "tkgd,skd->kgts", attended_grad, value_block, preferred_element_type=jnp.float32
        )
        score_grad = (weights_full * (weight_grad - row_delta[..., None])).astype(jnp.bfloat16)
        value_part = jnp.einsum(
            "kgts,tkgd->skd",
            weights_full.astype(jnp.bfloat16),
            attended_grad,
            preferred_element_type=jnp.float32,
        )
        key_part = (
            jnp.einsum("kgts,tkgd->skd", score_grad, query_four, preferred_element_type=jnp.float32)
            * factor
        )
        query_sum = (
            query_sum
            + jnp.einsum(
                "kgts,skd->tkgd", score_grad, key_block, preferred_element_type=jnp.float32
            )
            * factor
        )
        return (query_sum, (key_part, value_part))

    query_grad_rot, (key_parts, value_parts) = lax.scan(
        back_step,
        jnp.zeros((tokens, kv_heads, grouping, HD), jnp.float32),
        (key_blocks, value_blocks, id_blocks),
    )
    key_total, value_total = (
        lax.psum_scatter(
            key_parts.reshape(length, kv_heads * HD).astype(jnp.bfloat16),
            "ctx",
            scatter_dimension=0,
            tiled=True,
        ).astype(jnp.float32),
        lax.psum_scatter(
            value_parts.reshape(length, kv_heads * HD).astype(jnp.bfloat16),
            "ctx",
            scatter_dimension=0,
            tiled=True,
        ).astype(jnp.float32),
    )
    query_back = (
        rotate(query_grad_rot.reshape(tokens, kv_heads * grouping, HD), cosine, -sine_turn)
        .reshape(tokens, -1)
        .astype(jnp.bfloat16)
    )
    key_back = (
        rotate(key_total.reshape(tokens, kv_heads, HD), cosine, -sine_turn)
        .reshape(tokens, -1)
        .astype(jnp.bfloat16)
    )
    value_back = value_total.astype(jnp.bfloat16)
    query_grad = jnp.einsum("td,tc->dc", input_one, query_back, preferred_element_type=jnp.float32)
    key_grad = jnp.einsum("td,tc->dc", input_one, key_back, preferred_element_type=jnp.float32)
    value_grad = jnp.einsum("td,tc->dc", input_one, value_back, preferred_element_type=jnp.float32)
    one_partial = jnp.einsum("tc,dc->td", query_back, query_w, preferred_element_type=jnp.float32)
    one_partial = one_partial + jnp.einsum(
        "tc,dc->td", key_back, key_w, preferred_element_type=jnp.float32
    )
    one_partial = one_partial + jnp.einsum(
        "tc,dc->td", value_back, value_w, preferred_element_type=jnp.float32
    )
    input_one_grad = lax.psum(one_partial.astype(jnp.bfloat16), "tp").astype(jnp.float32)
    gain_one_grad = jnp.sum(input_one_grad * normed_one, axis=0)
    input_grad = hidden_grad + norm_back(input_one_grad, normed_one, scale_one, gain_one)
    shares = (
        lax.psum_scatter(
            gain_one_grad.astype(jnp.bfloat16), "fsdp", scatter_dimension=0, tiled=True
        ).astype(jnp.float32),
        lax.psum_scatter(
            query_grad.astype(jnp.bfloat16), "fsdp", scatter_dimension=0, tiled=True
        ).astype(jnp.float32),
        lax.psum_scatter(
            key_grad.astype(jnp.bfloat16), "fsdp", scatter_dimension=0, tiled=True
        ).astype(jnp.float32),
        lax.psum_scatter(
            value_grad.astype(jnp.bfloat16), "fsdp", scatter_dimension=0, tiled=True
        ).astype(jnp.float32),
        lax.psum_scatter(
            out_grad_t.astype(jnp.bfloat16), "fsdp", scatter_dimension=0, tiled=True
        ).astype(jnp.float32),
        lax.psum_scatter(
            gain_two_grad.astype(jnp.bfloat16), "fsdp", scatter_dimension=0, tiled=True
        ).astype(jnp.float32),
        lax.psum_scatter(
            gate_grad.astype(jnp.bfloat16), "fsdp", scatter_dimension=0, tiled=True
        ).astype(jnp.float32),
        lax.psum_scatter(
            up_grad.astype(jnp.bfloat16), "fsdp", scatter_dimension=0, tiled=True
        ).astype(jnp.float32),
        lax.psum_scatter(
            down_grad_t.astype(jnp.bfloat16), "fsdp", scatter_dimension=0, tiled=True
        ).astype(jnp.float32),
    )
    shares = (
        lax.psum(shares[0].astype(jnp.bfloat16), "ctx").astype(jnp.float32),
        lax.psum(shares[1].astype(jnp.bfloat16), "ctx").astype(jnp.float32),
        lax.psum(shares[2].astype(jnp.bfloat16), "ctx").astype(jnp.float32),
        lax.psum(shares[3].astype(jnp.bfloat16), "ctx").astype(jnp.float32),
        lax.psum(shares[4].astype(jnp.bfloat16), "ctx").astype(jnp.float32),
        lax.psum(shares[5].astype(jnp.bfloat16), "ctx").astype(jnp.float32),
        lax.psum(shares[6].astype(jnp.bfloat16), "ctx").astype(jnp.float32),
        lax.psum(shares[7].astype(jnp.bfloat16), "ctx").astype(jnp.float32),
        lax.psum(shares[8].astype(jnp.bfloat16), "ctx").astype(jnp.float32),
    )
    return (
        output[None],
        input_grad[None],
        shares[0],
        shares[1],
        shares[2],
        shares[3],
        shares[4].T,
        shares[5],
        shares[6],
        shares[7],
        shares[8].T,
    )


def solution(mesh):
    return jax.shard_map(
        local,
        mesh=mesh,
        in_specs=(
            P("fsdp", "ctx", None),
            P("fsdp", "ctx"),
            P("fsdp", "ctx"),
            P("fsdp", "ctx", None),
            P("fsdp"),
            P("fsdp", "tp"),
            P("fsdp", "tp"),
            P("fsdp", "tp"),
            P("tp", "fsdp"),
            P("fsdp"),
            P("fsdp", "tp"),
            P("fsdp", "tp"),
            P("tp", "fsdp"),
        ),
        out_specs=(
            P("fsdp", "ctx", None),
            P("fsdp", "ctx", None),
            P("fsdp"),
            P("fsdp", "tp"),
            P("fsdp", "tp"),
            P("fsdp", "tp"),
            P("tp", "fsdp"),
            P("fsdp"),
            P("fsdp", "tp"),
            P("fsdp", "tp"),
            P("tp", "fsdp"),
        ),
        check_vma=False,
    )
```

profile of v0, /device:TPU:0, one launch (start us, length us, event | category | flops | bytes accessed | tf_op | source)
XLA Modules:
  0.0 1577.6 jit_solution(1991943502405839874)
XLA Ops:
  8.8 11.5 all_gather.37
  29.2 14.4 all_gather.38
  44.3 10.7 all-gather
  56.2 13.0 all_gather.40
  70.9 13.8 all_gather.41
  95.1 19.0 %while.39 = (s32[]{:T(128)}, f32[2,8,256]{2,1,0:T(8,128)S(1)}, f32[2,8,256]{2,1,0:T(8,128)S(1)}, s32[2,512]{1,0:T(2,128)S(1)}, s32[1,256]{1,0:T(1,128)S(1)}, /*i...) while((s32[]{:T(128)}, f32[2,8,256]{2,1,0:T(8,128)S(1)}, ...), condition=%wide.region_4.5_spmd.clone, body=%wide.region_1.4_spmd.clone.sunk | while | flops 285364224 | bytes 18046072 | solution.py:119
  114.1 9.6 while.40
  151.5 113.6 %all-gather.13.cloned.1.call-done = bf16[2048,2816]{1,0:T(8,128)(2,1)} async-done(((bf16[512,2816]{1,0:T(8,128)(2,1)}), bf16[2048,2816]{1,0:T(8,128)(2,1)}) %all-gather.13.cloned.1.call-update) | async-done | bytes 11534352 | tf_op jit(solution)/shard_map/all_gather | solution.py:75
  274.4 106.3 %all-gather.15.cloned.1.call-done = bf16[2048,2816]{1,0:T(8,128)(2,1)} async-done(((bf16[512,2816]{1,0:T(8,128)(2,1)}), bf16[2048,2816]{1,0:T(8,128)(2,1)}) %all-gather.15.cloned.1.call-update) | async-done | bytes 11534352 | tf_op jit(solution)/shard_map/all_gather | solution.py:76
  389.7 106.5 %all-gather.17.cloned.1.call-done = bf16[2816,2048]{1,0:T(8,128)(2,1)} async-done(((bf16[2816,512]{1,0:T(8,128)(2,1)}), bf16[2816,2048]{1,0:T(8,128)(2,1)}) %all-gather.17.cloned.1.call-update) | async-done | bytes 11534352 | tf_op jit(solution)/shard_map/all_gather | solution.py:80
  496.3 11.5 multiply_convert_fusion
  523.4 19.7 %all-reduce.13.cloned.1.call-done = bf16[256,2048]{1,0:T(8,128)(2,1)} async-done(((bf16[256,2048]{1,0:T(8,128)(2,1)}), bf16[256,2048]{1,0:T(8,128)(2,1)}) %all-reduce.13.cloned.1.call-update) | async-done | bytes 1048592 | tf_op jit(solution)/shard_map/psum | solution.py:170
  553.5 35.6 %while.41 = (s32[]{:T(128)}, f32[256,2,8,64]{0,3,2,1:T(8,128)S(1)}, bf16[2,512,2,64]{1,3,2,0:T(8,128)(2,1)}, bf16[2,512,2,64]{1,3,2,0:T(8,128)(2,1)}, bf16[2,512...) while((s32[]{:T(128)}, f32[256,2,8,64]{0,3,2,1:T(8,128)S(1)}, ...), condition=%wide.region_13.14_spmd.clone, body=%wide.region_12.13_spmd.clone.sunk | while | flops 1362034688 | bytes 98753912 | solution.py:210
  593.2 18.9 %reduce-scatter.10.cloned.1.call-done = bf16[256,128]{0,1:T(8,128)(2,1)} async-done(((bf16[1024,128]{0,1:T(8,128)(2,1)}), bf16[256,128]{0,1:T(8,128)(2,1)}) %reduce-scatter.10.cloned.1.call-update) | async-done | bytes 65552 | tf_op jit(solution)/shard_map/reduce_scatter | solution.py:216
  614.5 18.4 %reduce-scatter.12.cloned.1.call-done = bf16[256,128]{0,1:T(8,128)(2,1)} async-done(((bf16[1024,128]{0,1:T(8,128)(2,1)}), bf16[256,128]{0,1:T(8,128)(2,1)}) %reduce-scatter.12.cloned.1.call-update) | async-done | bytes 65552 | tf_op jit(solution)/shard_map/reduce_scatter | solution.py:222
  686.6 56.1 %reduce-scatter.20.cloned.1.call-done = bf16[512,1024]{1,0:T(8,128)(2,1)} async-done(((bf16[2048,1024]{1,0:T(8,128)(2,1)}), bf16[512,1024]{1,0:T(8,128)(2,1)}) %reduce-scatter.20.cloned.1.call-update) | async-done | bytes 1048592 | tf_op jit(solution)/shard_map/reduce_scatter | solution.py:266
  742.7 56.5 %reduce-scatter.14.cloned.1.call-done = bf16[512,1024]{1,0:T(8,128)(2,1)} async-done(((bf16[2048,1024]{1,0:T(8,128)(2,1)}), bf16[512,1024]{1,0:T(8,128)(2,1)}) %reduce-scatter.14.cloned.1.call-update) | async-done | bytes 1048592 | tf_op jit(solution)/shard_map/reduce_scatter | solution.py:257
  799.2 115.1 %reduce-scatter.22.cloned.1.call-done = bf16[512,2816]{1,0:T(8,128)(2,1)} async-done(((bf16[2048,2816]{1,0:T(8,128)(2,1)}), bf16[512,2816]{1,0:T(8,128)(2,1)}) %reduce-scatter.22.cloned.1.call-update) | async-done | bytes 2883600 | tf_op jit(solution)/shard_map/reduce_scatter | solution.py:272
  914.3 115.1 %reduce-scatter.24.cloned.1.call-done = bf16[512,2816]{1,0:T(8,128)(2,1)} async-done(((bf16[2048,2816]{1,0:T(8,128)(2,1)}), bf16[512,2816]{1,0:T(8,128)(2,1)}) %reduce-scatter.24.cloned.1.call-update) | async-done | bytes 2883600 | tf_op jit(solution)/shard_map/reduce_scatter | solution.py:275
  1029.4 115.1 %reduce-scatter.26.cloned.1.call-done = bf16[512,2816]{0,1:T(8,128)(2,1)} async-done(((bf16[2048,2816]{0,1:T(8,128)(2,1)}), bf16[512,2816]{0,1:T(8,128)(2,1)}) %reduce-scatter.26.cloned.1.call-update) | async-done | bytes 2883600 | tf_op jit(solution)/shard_map/reduce_scatter | solution.py:278
  1146.4 22.2 %all-reduce.17.cloned.1.call-done = (bf16[256,2048]{1,0:T(8,128)(2,1)}, bf16[256,2048]{1,0:T(8,128)(2,1)}) async-done(((bf16[256,2048]{1,0:T(8,128)(2,1)}, bf16[256,2048]{1,0:T(8,128)(2,1)}), (bf16[256,2048]{1,0:T(8,128)(2,1)}, bf16[256,2048]{1,0:T(8,128)(2,1)})) %all-reduce.17.cloned.1.call-update) | async-done | bytes 2097168 | tf_op jit(solution)/shard_map/psum | solution.py:155
  1170.7 10.3 all-reduce.4
  1181.1 12.3 all-reduce.2
  1200.1 353.1 %all-reduce.15.cloned.1.call-done = (bf16[1024,512]{0,1:T(8,128)(2,1)}, bf16[512,1024]{1,0:T(8,128)(2,1)}, bf16[512,128]{1,0:T(8,128)(2,1)}, bf16[512,128]{1,0:T...) async-done(((bf16[1024,512]{0,1:T(8,128)(2,1)}, bf16[512,1024]{1,0:T(8,128)(2,1)}, bf16[512,128]{1,0:T(8,128)(2,1)}, ...) | async-done | bytes 11010064 | tf_op jit(solution)/shard_map/psum | solution.py:287
  (267 shorter events, 247.1 us)
Async XLA Ops:
  7.2 77.7 %all-gather.9.cloned.1.call-start = ((), (), s32[]{:S(2)}) async-start(), calls=%async_computation.9 | async-start | bytes 5242880 | tf_op jit(solution)/shard_map/all_gather | solution.py:71
  7.9 117.1 %all-gather.11.cloned.1.call-start = ((), (), s32[]{:S(2)}) async-start(), calls=%async_computation.10 | async-start | bytes 5242880 | tf_op jit(solution)/shard_map/all_gather | solution.py:79
  8.7 139.6 %all-reduce.11.cloned.1.call-start = ((), (), s32[]{:S(2)}) async-start(), calls=%async_computation.11 | async-start | bytes 2097152 | tf_op jit(solution)/shard_map/psum | solution.py:144
  28.4 63.0 %copy-start.29 = (f32[4,1,512]{2,1,0:T(1,128)}, f32[4,1,512]{2,1,0:T(1,128)S(1)}, u32[]{:S(2)}) copy-start(f32[4,1,512]{2,1,0:T(1,128)S(1)} %convert_element_type.277) | copy-start | bytes 24580
  28.7 62.7 %copy-start.41 = (f32[256]{0:T(256)}, f32[256]{0:T(256)S(1)}, u32[]{:S(2)}) copy-start(f32[256]{0:T(256)S(1)} %add_rsqrt_fusion.1) | copy-start | bytes 3076
  28.7 27.4 %copy-start.37 = (bf16[512,128]{1,0:T(8,128)(2,1)S(1)}, bf16[512,128]{1,0:T(8,128)(2,1)}, u32[]{:S(2)}) copy-start(bf16[512,128]{1,0:T(8,128)(2,1)} %param.25) | copy-start | bytes 393220
  129.7 135.4 %all-gather.13.cloned.1.call-start = ((), (), s32[]{:S(2)}) async-start(), calls=%async_computation.12 | async-start | bytes 14417920 | tf_op jit(solution)/shard_map/all_gather | solution.py:75
  130.3 250.5 %all-gather.15.cloned.1.call-start = ((), (), s32[]{:S(2)}) async-start(), calls=%async_computation.13 | async-start | bytes 14417920 | tf_op jit(solution)/shard_map/all_gather | solution.py:76
  130.9 365.4 %all-gather.17.cloned.1.call-start = ((), (), s32[]{:S(2)}) async-start(), calls=%async_computation.14 | async-start | bytes 14417920 | tf_op jit(solution)/shard_map/all_gather | solution.py:80
  131.5 411.6 %all-reduce.13.cloned.1.call-start = ((), (), s32[]{:S(2)}) async-start(), calls=%async_computation.15 | async-start | bytes 2097152 | tf_op jit(solution)/shard_map/psum | solution.py:170
  151.5 229.2 %copy-start.6 = (bf16[256,2048]{1,0:T(8,128)(2,1)S(1)}, bf16[256,2048]{1,0:T(8,128)(2,1)}, u32[]{:S(2)}) copy-start(bf16[256,2048]{1,0:T(8,128)(2,1)} %multiply_convert_fusion.3) | copy-start | bytes 3145732
  523.3 88.8 %reduce-scatter.10.cloned.1.call-start = ((), (), s32[]{:S(2)}) async-start(), calls=%async_computation.16 | async-start | bytes 327680 | tf_op jit(solution)/shard_map/reduce_scatter | solution.py:216
  591.1 41.9 %reduce-scatter.12.cloned.1.call-start = ((), (), s32[]{:S(2)}) async-start(), calls=%async_computation.17 | async-start | bytes 327680 | tf_op jit(solution)/shard_map/reduce_scatter | solution.py:222
  593.1 90.7 %reduce-scatter.16.cloned.1.call-start = ((), (), s32[]{:S(2)}) async-start(), calls=%async_computation.19 | async-start | bytes 655360 | tf_op jit(solution)/shard_map/reduce_scatter | solution.py:260
  614.5 72.1 %reduce-scatter.18.cloned.1.call-start = ((), (), s32[]{:S(2)}) async-start(), calls=%async_computation.20 | async-start | bytes 655360 | tf_op jit(solution)/shard_map/reduce_scatter | solution.py:263
  635.2 107.5 %reduce-scatter.20.cloned.1.call-start = ((), (), s32[]{:S(2)}) async-start(), calls=%async_computation.21 | async-start | bytes 5242880 | tf_op jit(solution)/shard_map/reduce_scatter | solution.py:266
  641.3 157.9 %reduce-scatter.14.cloned.1.call-start = ((), (), s32[]{:S(2)}) async-start(), calls=%async_computation.18 | async-start | bytes 5242880 | tf_op jit(solution)/shard_map/reduce_scatter | solution.py:257
  645.0 269.3 %reduce-scatter.22.cloned.1.call-start = ((), (), s32[]{:S(2)}) async-start(), calls=%async_computation.22 | async-start | bytes 14417920 | tf_op jit(solution)/shard_map/reduce_scatter | solution.py:272
  653.8 375.6 %reduce-scatter.24.cloned.1.call-start = ((), (), s32[]{:S(2)}) async-start(), calls=%async_computation.23 | async-start | bytes 14417920 | tf_op jit(solution)/shard_map/reduce_scatter | solution.py:275
  661.2 483.4 %reduce-scatter.26.cloned.1.call-start = ((), (), s32[]{:S(2)}) async-start(), calls=%async_computation.24 | async-start | bytes 14417920 | tf_op jit(solution)/shard_map/reduce_scatter | solution.py:278
  669.8 498.8 %all-reduce.17.cloned.1.call-start = ((), (), s32[]{:S(2)}) async-start(), calls=%async_computation.26 | async-start | bytes 4194304 | tf_op jit(solution)/shard_map/psum | solution.py:155
  683.7 869.4 %all-reduce.15.cloned.1.call-start = ((), (), s32[]{:S(2)}) async-start(), calls=%async_computation.25 | async-start | bytes 22020096 | tf_op jit(solution)/shard_map/psum | solution.py:287
  1144.5 26.1 %copy-start.43 = (bf16[2048]{0:T(1024)(128)(2,1)S(1)}, bf16[2048]{0:T(1024)(128)(2,1)}, u32[]{:S(2)}) copy-start(bf16[2048]{0:T(1024)(128)(2,1)} %get-tuple-element.380) | copy-start | bytes 12292
  1144.6 50.0 %copy-start.5 = (bf16[256,2048]{1,0:T(8,128)(2,1)S(1)}, bf16[256,2048]{1,0:T(8,128)(2,1)}, u32[]{:S(2)}) copy-start(bf16[256,2048]{1,0:T(8,128)(2,1)} %all-reduce.11.cloned.1.call-done) | copy-start | bytes 3145732
  (49 other events, 360.6 us)
Sparse Core Ops, SparseCore 0:
  9.9 59.6 all-gather.8
  71.4 52.5 all-gather.10
  129.8 18.3 all-reduce.10
  150.1 114.9 all-gather.12
  266.9 113.7 all-gather.14
  382.6 113.6 all-gather.16
  523.4 19.5 all-reduce.12
  591.2 20.8 reduce-scatter.9
  615.0 17.8 reduce-scatter.11
  635.6 23.0 reduce-scatter.15
  661.8 24.7 reduce-scatter.17
  690.0 52.6 reduce-scatter.19
  746.5 52.6 reduce-scatter.13
  802.2 112.1 reduce-scatter.21
  917.3 112.0 reduce-scatter.23
  1032.4 112.0 reduce-scatter.25
  1147.3 21.2 all-reduce.16
  1172.3 380.7 all-reduce.14
where the time goes:
time: 1590 us; the launch traced here: 1580 us
  waiting for transfers between devices  1230 us (77%)
  matrix products  157 us (10%)
  blocking collectives  102 us (6%)
  other arithmetic  46.7 us (3%)
  local copies, waits for them, and re-layouts  23.8 us (1%)
  between operations  16 us (1%)
    psum x1, waiting for transfers between devices, local(): lax.psum(shares[4].astype(jnp.bfloat16), 'ctx').astype(jnp.float32)  353 us
    reduce_scatter x1, waiting for transfers between devices, local(): lax.psum_scatter(gate_grad.astype(jnp.bfloat16), 'fsdp', scatter_dimensio...  115 us
    reduce_scatter x1, waiting for transfers between devices, local(): lax.psum_scatter(down_grad_t.astype(jnp.bfloat16), 'fsdp', scatter_dimens...  115 us
    reduce_scatter x1, waiting for transfers between devices, local(): lax.psum_scatter(up_grad.astype(jnp.bfloat16), 'fsdp', scatter_dimension=...  115 us
    all_gather x1, waiting for transfers between devices, local(): lax.all_gather(w_gate, 'fsdp', axis=0, tiled=True)  114 us
    all_gather x1, waiting for transfers between devices, local(): lax.all_gather(w_down, 'fsdp', axis=1, tiled=True)  107 us
    all_gather x1, waiting for transfers between devices, local(): lax.all_gather(w_up, 'fsdp', axis=0, tiled=True)  106 us
    reduce_scatter x1, waiting for transfers between devices, local(): lax.psum_scatter(query_grad.astype(jnp.bfloat16), 'fsdp', scatter_dimensi...  56.5 us
  transfers between devices with their start and end apart: 18, of which 15 were waited for; matrix products, arithmetic and copies ran while one was open for 8% of the time, Pallas kernels for 0%

commit v1 on v0

--- a/solution.py
+++ b/solution.py
@@ -284,7 +284,7 @@
         lax.psum(shares[1].astype(jnp.bfloat16), "ctx").astype(jnp.float32),
         lax.psum(shares[2].astype(jnp.bfloat16), "ctx").astype(jnp.float32),
         lax.psum(shares[3].astype(jnp.bfloat16), "ctx").astype(jnp.float32),
-        lax.psum(shares[4].astype(jnp.bfloat16), "ctx").astype(jnp.float32),
+        jnp.sum(lax.all_gather(shares[4].astype(jnp.bfloat16), "ctx"), axis=0).astype(jnp.float32),
         lax.psum(shares[5].astype(jnp.bfloat16), "ctx").astype(jnp.float32),
         lax.psum(shares[6].astype(jnp.bfloat16), "ctx").astype(jnp.float32),
         lax.psum(shares[7].astype(jnp.bfloat16), "ctx").astype(jnp.float32),

time: 1590 us -> 1640 us (1.031)
  waiting for transfers between devices: 1230 us -> 1270 us
    all_gather x0 -> x1, waiting for transfers between devices: none -> 52.6 us  [local(): lax.all_gather(shares[4].astype(jnp.bfloat16), 'ctx')]
    reduce_scatter x1, waiting for transfers between devices: 56.1 us -> 10.4 us  [local(): lax.psum_scatter(out_grad_t.astype(jnp.bfloat16), 'fsdp', scatter_dimensi...]
    reduce_scatter x1, waiting for transfers between devices: 0.02 us -> 27.8 us  [local(): lax.psum_scatter(key_grad.astype(jnp.bfloat16), 'fsdp', scatter_dimension...]
    reduce_scatter x1, waiting for transfers between devices: 2.77 us -> 27.5 us  [local(): lax.psum_scatter(value_grad.astype(jnp.bfloat16), 'fsdp', scatter_dimensi...]
  transfers between devices with their start and end apart: 18 -> 19, of which waited for: 15 -> 17; matrix products, arithmetic and copies ran while one was open for 8% -> 8% of each run, Pallas kernels for 0% -> 0%
where the time goes in v1:
time: 1640 us; the launch traced here: 1630 us
  waiting for transfers between devices  1270 us (77%)
  matrix products  152 us (9%)
  blocking collectives  104 us (6%)
  other arithmetic  46.9 us (3%)
  local copies, waits for them, and re-layouts  33.8 us (2%)
    psum x1, waiting for transfers between devices, local(): lax.psum(shares[1].astype(jnp.bfloat16), 'ctx').astype(jnp.float32)  342 us
    reduce_scatter x1, waiting for transfers between devices, local(): lax.psum_scatter(gate_grad.astype(jnp.bfloat16), 'fsdp', scatter_dimensio...  115 us
    reduce_scatter x1, waiting for transfers between devices, local(): lax.psum_scatter(down_grad_t.astype(jnp.bfloat16), 'fsdp', scatter_dimens...  115 us
    reduce_scatter x1, waiting for transfers between devices, local(): lax.psum_scatter(up_grad.astype(jnp.bfloat16), 'fsdp', scatter_dimension=...  115 us
    all_gather x1, waiting for transfers between devices, local(): lax.all_gather(w_gate, 'fsdp', axis=0, tiled=True)  115 us
    all_gather x1, waiting for transfers between devices, local(): lax.all_gather(w_up, 'fsdp', axis=0, tiled=True)  107 us
    all_gather x1, waiting for transfers between devices, local(): lax.all_gather(w_down, 'fsdp', axis=1, tiled=True)  107 us
    reduce_scatter x1, waiting for transfers between devices, local(): lax.psum_scatter(query_grad.astype(jnp.bfloat16), 'fsdp', scatter_dimensi...  56.5 us
  transfers between devices with their start and end apart: 19, of which 17 were waited for; matrix products, arithmetic and copies ran while one was open for 8% of the time, Pallas kernels for 0%

profile of v1, /device:TPU:0, one launch (start us, length us, event | category | flops | bytes accessed | tf_op | source)
XLA Modules:
  0.0 1628.4 jit_solution(8851682597219578639)
XLA Ops:
  18.7 14.8 all_gather.46
  37.0 14.2 all_gather.47
  53.0 10.9 all-gather
  65.1 10.5 all_gather.43
  77.0 13.9 all_gather.44
  101.8 18.7 %while.39 = (s32[]{:T(128)}, f32[2,8,256]{2,1,0:T(8,128)S(1)}, f32[2,8,256]{2,1,0:T(8,128)S(1)}, s32[2,512]{1,0:T(2,128)S(1)}, s32[1,256]{1,0:T(1,128)S(1)}, /*i...) while((s32[]{:T(128)}, f32[2,8,256]{2,1,0:T(8,128)S(1)}, ...), condition=%wide.region_4.5_spmd.clone, body=%wide.region_1.4_spmd.clone.sunk | while | flops 285364224 | bytes 18046064 | solution.py:119
  153.1 114.6 %all-gather.15.cloned.1.call-done = bf16[2048,2816]{1,0:T(8,128)(2,1)} async-done(((bf16[512,2816]{1,0:T(8,128)(2,1)}), bf16[2048,2816]{1,0:T(8,128)(2,1)}) %all-gather.15.cloned.1.call-update) | async-done | bytes 11534352 | tf_op jit(solution)/shard_map/all_gather | solution.py:75
  276.7 106.7 %all-gather.17.cloned.1.call-done = bf16[2048,2816]{1,0:T(8,128)(2,1)} async-done(((bf16[512,2816]{1,0:T(8,128)(2,1)}), bf16[2048,2816]{1,0:T(8,128)(2,1)}) %all-gather.17.cloned.1.call-update) | async-done | bytes 11534352 | tf_op jit(solution)/shard_map/all_gather | solution.py:76
  392.3 106.5 %all-gather.19.cloned.1.call-done = bf16[2816,2048]{1,0:T(8,128)(2,1)} async-done(((bf16[2816,512]{1,0:T(8,128)(2,1)}), bf16[2816,2048]{1,0:T(8,128)(2,1)}) %all-gather.19.cloned.1.call-update) | async-done | bytes 11534352 | tf_op jit(solution)/shard_map/all_gather | solution.py:80
  498.8 11.4 multiply_convert_fusion
  525.9 19.7 %all-reduce.13.cloned.1.call-done = bf16[256,2048]{1,0:T(8,128)(2,1)} async-done(((bf16[256,2048]{1,0:T(8,128)(2,1)}), bf16[256,2048]{1,0:T(8,128)(2,1)}) %all-reduce.13.cloned.1.call-update) | async-done | bytes 1048592 | tf_op jit(solution)/shard_map/psum | solution.py:170
  556.1 40.7 %while.41 = (s32[]{:T(128)}, f32[256,2,8,64]{0,3,2,1:T(8,128)S(1)}, bf16[2,512,2,64]{1,3,2,0:T(8,128)(2,1)}, bf16[2,512,2,64]{1,3,2,0:T(8,128)(2,1)}, bf16[2,512...) while((s32[]{:T(128)}, f32[256,2,8,64]{0,3,2,1:T(8,128)S(1)}, ...), condition=%wide.region_13.14_spmd.clone, body=%wide.region_12.13_spmd.clone.sunk | while | flops 1362034688 | bytes 96657208 | solution.py:210
  607.0 12.7 reduce-scatter.10.cloned.1.call-done
  622.2 18.5 %reduce-scatter.12.cloned.1.call-done = bf16[256,128]{0,1:T(8,128)(2,1)} async-done(((bf16[1024,128]{0,1:T(8,128)(2,1)}), bf16[256,128]{0,1:T(8,128)(2,1)}) %reduce-scatter.12.cloned.1.call-update) | async-done | bytes 65552 | tf_op jit(solution)/shard_map/reduce_scatter | solution.py:222
  695.2 27.8 %reduce-scatter.16.cloned.1.call-done = bf16[512,128]{1,0:T(8,128)(2,1)} async-done(((bf16[2048,128]{1,0:T(8,128)(2,1)}), bf16[512,128]{1,0:T(8,128)(2,1)}) %reduce-scatter.16.cloned.1.call-update) | async-done | bytes 131088 | tf_op jit(solution)/shard_map/reduce_scatter | solution.py:260
  723.0 27.5 %reduce-scatter.18.cloned.1.call-done = bf16[512,128]{1,0:T(8,128)(2,1)} async-done(((bf16[2048,128]{1,0:T(8,128)(2,1)}), bf16[512,128]{1,0:T(8,128)(2,1)}) %reduce-scatter.18.cloned.1.call-update) | async-done | bytes 131088 | tf_op jit(solution)/shard_map/reduce_scatter | solution.py:263
  750.5 56.5 %reduce-scatter.14.cloned.1.call-done = bf16[512,1024]{1,0:T(8,128)(2,1)} async-done(((bf16[2048,1024]{1,0:T(8,128)(2,1)}), bf16[512,1024]{1,0:T(8,128)(2,1)}) %reduce-scatter.14.cloned.1.call-update) | async-done | bytes 1048592 | tf_op jit(solution)/shard_map/reduce_scatter | solution.py:257
  807.0 115.1 %reduce-scatter.22.cloned.1.call-done = bf16[512,2816]{1,0:T(8,128)(2,1)} async-done(((bf16[2048,2816]{1,0:T(8,128)(2,1)}), bf16[512,2816]{1,0:T(8,128)(2,1)}) %reduce-scatter.22.cloned.1.call-update) | async-done | bytes 2883600 | tf_op jit(solution)/shard_map/reduce_scatter | solution.py:272
  922.1 115.1 %reduce-scatter.24.cloned.1.call-done = bf16[512,2816]{1,0:T(8,128)(2,1)} async-done(((bf16[2048,2816]{1,0:T(8,128)(2,1)}), bf16[512,2816]{1,0:T(8,128)(2,1)}) %reduce-scatter.24.cloned.1.call-update) | async-done | bytes 2883600 | tf_op jit(solution)/shard_map/reduce_scatter | solution.py:275
  1037.2 115.1 %reduce-scatter.26.cloned.1.call-done = bf16[512,2816]{0,1:T(8,128)(2,1)} async-done(((bf16[2048,2816]{0,1:T(8,128)(2,1)}), bf16[512,2816]{0,1:T(8,128)(2,1)}) %reduce-scatter.26.cloned.1.call-update) | async-done | bytes 2883600 | tf_op jit(solution)/shard_map/reduce_scatter | solution.py:278
  1154.2 22.2 %all-reduce.17.cloned.1.call-done = (bf16[256,2048]{1,0:T(8,128)(2,1)}, bf16[256,2048]{1,0:T(8,128)(2,1)}) async-done(((bf16[256,2048]{1,0:T(8,128)(2,1)}, bf16[256,2048]{1,0:T(8,128)(2,1)}), (bf16[256,2048]{1,0:T(8,128)(2,1)}, bf16[256,2048]{1,0:T(8,128)(2,1)})) %all-reduce.17.cloned.1.call-update) | async-done | bytes 2097168 | tf_op jit(solution)/shard_map/psum | solution.py:155
  1188.9 12.2 all-reduce.2
  1207.5 52.6 %all-gather.21.cloned.1.call-done = bf16[2048,1024]{1,0:T(8,128)(2,1)} async-done(((bf16[512,1024]{1,0:T(8,128)(2,1)}), bf16[2048,1024]{1,0:T(8,128)(2,1)}) %all-gather.21.cloned.1.call-update) | async-done | bytes 4194320 | tf_op jit(solution)/shard_map/all_gather | solution.py:287
  1265.5 341.7 %all-reduce.15.cloned.1.call-done = (bf16[512,1024]{1,0:T(8,128)(2,1)}, bf16[512,128]{1,0:T(8,128)(2,1)}, bf16[512,128]{1,0:T(8,128)(2,1)}, bf16[512,2816]{1,0:T...) async-done(((bf16[512,1024]{1,0:T(8,128)(2,1)}, bf16[512,128]{1,0:T(8,128)(2,1)}, bf16[512,128]{1,0:T(8,128)(2,1)}, bf16[512,2816]{1,0:T(8,128)(2,1)}, ...) | async-done | bytes 9961488 | tf_op jit(solution)/shard_map/psum | solution.py:284
  (282 shorter events, 278.5 us)
Async XLA Ops:
  7.2 84.3 %all-gather.11.cloned.1.call-start = ((), (), s32[]{:S(2)}) async-start(), calls=%async_computation.9 | async-start | bytes 5242880 | tf_op jit(solution)/shard_map/all_gather | solution.py:71
  8.0 120.1 %all-gather.13.cloned.1.call-start = ((), (), s32[]{:S(2)}) async-start(), calls=%async_computation.10 | async-start | bytes 5242880 | tf_op jit(solution)/shard_map/all_gather | solution.py:79
  8.7 142.1 %all-reduce.11.cloned.1.call-start = ((), (), s32[]{:S(2)}) async-start(), calls=%async_computation.11 | async-start | bytes 2097152 | tf_op jit(solution)/shard_map/psum | solution.py:144
  18.4 79.6 %copy-start.32 = (f32[4,1,512]{2,1,0:T(1,128)}, f32[4,1,512]{2,1,0:T(1,128)S(1)}, u32[]{:S(2)}) copy-start(f32[4,1,512]{2,1,0:T(1,128)S(1)} %convert_element_type.288) | copy-start | bytes 24580
  18.7 79.3 %copy-start.43 = (f32[256]{0:T(256)}, f32[256]{0:T(256)S(1)}, u32[]{:S(2)}) copy-start(f32[256]{0:T(256)S(1)} %add_rsqrt_fusion.1) | copy-start | bytes 3076
  35.3 66.3 %copy-start.28 = (f32[256,32]{0,1:T(8,128)}, f32[256,32]{0,1:T(8,128)S(1)}, u32[]{:S(2)}) copy-start(f32[256,32]{0,1:T(8,128)S(1)} %get-tuple-element.449) | copy-start | bytes 98308
  132.7 134.9 %all-gather.15.cloned.1.call-start = ((), (), s32[]{:S(2)}) async-start(), calls=%async_computation.12 | async-start | bytes 14417920 | tf_op jit(solution)/shard_map/all_gather | solution.py:75
  133.3 250.0 %all-gather.17.cloned.1.call-start = ((), (), s32[]{:S(2)}) async-start(), calls=%async_computation.13 | async-start | bytes 14417920 | tf_op jit(solution)/shard_map/all_gather | solution.py:76
  133.9 364.9 %all-gather.19.cloned.1.call-start = ((), (), s32[]{:S(2)}) async-start(), calls=%async_computation.14 | async-start | bytes 14417920 | tf_op jit(solution)/shard_map/all_gather | solution.py:80
  134.5 411.1 %all-reduce.13.cloned.1.call-start = ((), (), s32[]{:S(2)}) async-start(), calls=%async_computation.15 | async-start | bytes 2097152 | tf_op jit(solution)/shard_map/psum | solution.py:170
  152.5 448.4 %copy-start.46 = (f32[256]{0:T(256)}, f32[256]{0:T(256)S(1)}, u32[]{:S(2)}) copy-start(f32[256]{0:T(256)S(1)} %add_rsqrt_fusion) | copy-start | bytes 3076
  153.1 230.3 %copy-start.6 = (bf16[256,2048]{1,0:T(8,128)(2,1)}, bf16[256,2048]{1,0:T(8,128)(2,1)S(1)}, u32[]{:S(2)}) copy-start(bf16[256,2048]{1,0:T(8,128)(2,1)S(1)} %multiply_convert_fusion.3) | copy-start | bytes 3145732
  525.8 93.9 %reduce-scatter.10.cloned.1.call-start = ((), (), s32[]{:S(2)}) async-start(), calls=%async_computation.16 | async-start | bytes 327680 | tf_op jit(solution)/shard_map/reduce_scatter | solution.py:216
  598.8 41.9 %reduce-scatter.12.cloned.1.call-start = ((), (), s32[]{:S(2)}) async-start(), calls=%async_computation.17 | async-start | bytes 327680 | tf_op jit(solution)/shard_map/reduce_scatter | solution.py:222
  600.9 94.3 %reduce-scatter.20.cloned.1.call-start = ((), (), s32[]{:S(2)}) async-start(), calls=%async_computation.21 | async-start | bytes 5242880 | tf_op jit(solution)/shard_map/reduce_scatter | solution.py:266
  607.0 116.0 %reduce-scatter.16.cloned.1.call-start = ((), (), s32[]{:S(2)}) async-start(), calls=%async_computation.19 | async-start | bytes 655360 | tf_op jit(solution)/shard_map/reduce_scatter | solution.py:260
  622.1 128.3 %reduce-scatter.18.cloned.1.call-start = ((), (), s32[]{:S(2)}) async-start(), calls=%async_computation.20 | async-start | bytes 655360 | tf_op jit(solution)/shard_map/reduce_scatter | solution.py:263
  643.0 164.0 %reduce-scatter.14.cloned.1.call-start = ((), (), s32[]{:S(2)}) async-start(), calls=%async_computation.18 | async-start | bytes 5242880 | tf_op jit(solution)/shard_map/reduce_scatter | solution.py:257
  647.5 274.6 %reduce-scatter.22.cloned.1.call-start = ((), (), s32[]{:S(2)}) async-start(), calls=%async_computation.22 | async-start | bytes 14417920 | tf_op jit(solution)/shard_map/reduce_scatter | solution.py:272
  655.6 381.6 %reduce-scatter.24.cloned.1.call-start = ((), (), s32[]{:S(2)}) async-start(), calls=%async_computation.23 | async-start | bytes 14417920 | tf_op jit(solution)/shard_map/reduce_scatter | solution.py:275
  663.1 489.3 %reduce-scatter.26.cloned.1.call-start = ((), (), s32[]{:S(2)}) async-start(), calls=%async_computation.24 | async-start | bytes 14417920 | tf_op jit(solution)/shard_map/reduce_scatter | solution.py:278
  671.7 504.7 %all-reduce.17.cloned.1.call-start = ((), (), s32[]{:S(2)}) async-start(), calls=%async_computation.27 | async-start | bytes 4194304 | tf_op jit(solution)/shard_map/psum | solution.py:155
  684.7 575.4 %all-gather.21.cloned.1.call-start = ((), (), s32[]{:S(2)}) async-start(), calls=%async_computation.25 | async-start | bytes 5242880 | tf_op jit(solution)/shard_map/all_gather | solution.py:287
  695.2 912.0 %all-reduce.15.cloned.1.call-start = ((), (), s32[]{:S(2)}) async-start(), calls=%async_computation.26 | async-start | bytes 19922944 | tf_op jit(solution)/shard_map/psum | solution.py:284
  (55 other events, 521.5 us)
Sparse Core Ops, SparseCore 0:
  9.9 61.2 all-gather.10
  73.1 53.3 all-gather.12
  132.8 17.9 all-reduce.10
  152.6 114.9 all-gather.14
  269.5 113.7 all-gather.16
  385.1 113.6 all-gather.18
  526.0 19.5 all-reduce.12
  599.0 20.7 reduce-scatter.9
  622.7 17.9 reduce-scatter.11
  644.1 51.0 reduce-scatter.19
  698.2 24.7 reduce-scatter.15
  725.7 24.7 reduce-scatter.17
  754.3 52.6 reduce-scatter.13
  810.0 112.1 reduce-scatter.21
  925.1 112.0 reduce-scatter.23
  1040.2 112.0 reduce-scatter.25
  1155.1 21.2 all-reduce.16
  1177.9 82.1 all-gather.20
  1263.7 343.4 all-reduce.14
